TPU v7x, 256 devices: a whole 4x4x8 slice. The times are simulated.
256 devices in a mesh: prow: 16 (over y_hi, z), pcol: 16 (over x, y_lo, core).
Axes of the slice: x: 4, y: 4 (y_hi: 2, y_lo: 2; y = y_hi * 2 + y_lo), z: 8, core: 2. Of those that a mesh axis runs over, the one named last changes fastest.
Arguments:
- ainv: float32 [20480, 20480], P('prow', 'pcol'), may hold values from -0.15625 to 0.15625
- panels: float32 [3, 20480, 512], P(None, ('prow', 'pcol')), may hold values from -0.8 to 0.8
- ancestors: int32 [3, 2560], P(None, ('prow', 'pcol')), may hold values from 0 to 1, as said below
- dinv: float32 [3, 512, 512], P(None, 'prow', 'pcol'), may hold values from -6 to 6
Outputs:
- u_panel: float32 [3, 20480, 512], P(None, ('prow', 'pcol'))
- diag: float32 [3, 512, 512], P(None, 'prow', 'pcol')
Inputs may be any that keep to these rules, and one draw needn't show every extreme that they name: `ancestors`: each entry is 0 or 1; the share of ancestor blocks varies strongly between regions of the rows.
All inputs are finite; a program needn't handle non-finite values.
Results may differ from a plain program's by a relative error of at most 0.00007.
Values sent between devices are 32-bit elements; how exact they have to be, the bound alone decides.
A program may use at most 128 MiB of HBM per device.

v0:
```python
import jax
import jax.numpy as jnp
from jax import lax
from jax.sharding import Mesh
from jax.sharding import PartitionSpec as P

S = 512
NSUP = 3
BLK = 8
PCOL = ("pcol_0", "pcol_1", "pcol_2")
PROW_PCOL = ("prow", "pcol_0", "pcol_1", "pcol_2")


def split_up(value, dim, peers):
    before, after = (value.shape[:dim], value.shape[dim + 1 :])
    return jnp.moveaxis(value.reshape(*before, peers, -1, *after), dim, 0)


def sum_by_chip(value, chips, core, dim):
    sizes = (lax.axis_size(chips), lax.axis_size(core))
    tiles = split_up(value, dim, sizes[0] * sizes[1])
    inside = tiles.shape[1:]
    tiles = tiles.reshape(*sizes, *inside).swapaxes(0, 1).reshape(-1, *inside)
    tiles = lax.psum_scatter(tiles, core, scatter_dimension=0, tiled=True)
    return lax.psum_scatter(tiles, chips, scatter_dimension=0, tiled=True)[0]


def sent_and_summed(value, axis, dim):
    peers = lax.axis_size(axis)
    tiles = lax.all_to_all(split_up(value, dim, peers), axis, 0, 0, tiled=True)
    return jnp.sum(tiles, axis=0)


def apply_rows(columns, piece):

    def dense_product():
        return jnp.dot(columns, piece, precision=lax.Precision.HIGHEST)

    def no_product():
        return jnp.zeros((columns.shape[0], piece.shape[1]), jnp.float32)

    return lax.cond(jnp.any(piece != 0.0), dense_product, no_product)


def on_device(ainv, panels, ancestors, dinv):
    row_flags = jnp.repeat(ancestors, BLK, axis=1).astype(jnp.float32)
    masked = panels * row_flags[:, :, None]
    local_rows = ainv.shape[0]
    empty = jnp.zeros((NSUP, local_rows, S), jnp.float32)
    total = empty
    piece = lax.all_gather(masked, "prow", axis=1, tiled=True)
    for member in range(NSUP):
        total = total.at[member].add(apply_rows(ainv, piece[member]))
    partial_value = sum_by_chip(total, ("pcol_0", "pcol_1"), "pcol_2", 1)
    u_panel = -(row_flags[:, :, None] * partial_value)
    local_terms = jnp.einsum("srn,srm->snm", masked, u_panel, precision=lax.Precision.HIGHEST)
    by_columns = sent_and_summed(local_terms, PCOL, 2)
    own_block = sent_and_summed(by_columns, "prow", 1)
    diag = dinv - own_block
    return (u_panel, diag)


def solution(mesh):
    split = Mesh(
        mesh.devices.reshape(mesh.shape["prow"], 4, 2, 2), ("prow", "pcol_0", "pcol_1", "pcol_2")
    )
    in_specs = (
        P("prow", PCOL),
        P(None, PROW_PCOL, None),
        P(None, PROW_PCOL),
        P(None, "prow", PCOL),
    )
    out_specs = (P(None, PROW_PCOL, None), P(None, "prow", PCOL))
    return jax.shard_map(
        on_device, mesh=split, in_specs=in_specs, out_specs=out_specs, check_vma=False
    )
```

profile of v0, /device:TPU:32, one launch (start us, length us, event | category | flops | bytes accessed | tf_op | source)
XLA Modules:
  0.0 404.4 jit_solution(11009436670930716270)
XLA Ops:
  7.2 0.7 convert_element_type.20
  8.1 1.9 broadcast_multiply_fusion
  10.0 132.6 %all-gather.2.cloned.1.call-done = f32[3,1280,512]{2,1,0:T(8,128)} async-done(((f32[3,80,512]{2,1,0:T(8,128)}), f32[3,1280,512]{2,1,0:T(8,128)}) %all-gather.2.cloned.1.call-update) | async-done | bytes 7864336 | tf_op jit(solution)/shard_map/all_gather | solution.py:51
  142.6 5.0 %compare_reduce_fusion = (pred[]{:T(512)}, pred[]{:T(512)}, pred[]{:T(512)}) fusion(f32[3,1280,512]{2,1,0:T(8,128)} %all-gather.2.cloned.1.call-done), kind=kLoop, calls=%fused_computation.9 | loop fusion | flops 3932157 | bytes 7864323 | tf_op jit(solution)/shard_map/reduce_or | solution.py:42
  149.6 6.7 %slice_bitcast_fusion = (f32[1280,512]{1,0:T(8,128)}, f32[1280,512]{1,0:T(8,128)}, f32[1280,512]{1,0:T(8,128)}) fusion(f32[3,1280,512]{2,1,0:T(8,128)} %all-gather.2.cloned.1.call-done), kind=kLoop, calls=%fused_computation.4 | loop fusion | bytes 15728640 | tf_op jit(solution)/shard_map/squeeze | solution.py:53
  156.2 13.4 %conditional.4 = (f32[1,1280,512]{2,1,0:T(8,128)S(1)}) conditional(s32[]{:T(128)} %convert_element_type.23, () %tuple.46, (f32[1280,1280]{1,0:T(8,128)}, f32[1280,512]{1,0:T(8,128)}) %tuple.47), branch_computations={%region_4.0_spmd, %region_5.0_spmd} | conditional | flops 10066329600 | bytes 11796488 | solution.py:42
  156.2 13.4 %convolution_bitcast_fusion.1 = f32[1,1280,512]{2,1,0:T(8,128)S(1)} fusion(f32[1280,1280]{1,0:T(8,128)} %get-tuple-element.62, f32[1280,512]{1,0:T(8,128)} %get-tuple-element.63), kind=kOutput, calls=%fused_computation.1 | convolution fusion | flops 10066329600 | bytes 11796480 | tf_op jit(solution)/shard_map/cond/branch_1_fun/dot_general | solution.py:37
  169.6 17.6 %conditional.3 = (f32[3,1280,512]{2,1,0:T(8,128)}) conditional(s32[]{:T(128)} %convert_element_type.22, () %tuple.44, (f32[1280,1280]{1,0:T(8,128)}, f32[1280,512]{1,0:T(8,128)}) %tuple.45), branch_computations={%region_1.0_spmd, %region_2.0_spmd} | conditional | flops 10066329600 | bytes 22282252 | solution.py:42
  169.8 13.4 %convolution_bitcast_fusion = f32[1,1280,512]{2,1,0:T(8,128)S(1)} fusion(f32[1280,1280]{1,0:T(8,128)} %get-tuple-element.60, f32[1280,512]{1,0:T(8,128)} %get-tuple-element.61), kind=kOutput, calls=%fused_computation | convolution fusion | flops 10066329600 | bytes 11796480 | tf_op jit(solution)/shard_map/cond/branch_1_fun/dot_general | solution.py:37
  183.3 4.0 scatter-add.9
  187.3 1.8 constant_dynamic-update-slice_fusion
  189.0 13.4 %conditional.5 = (f32[1,1280,512]{2,1,0:T(8,128)S(1)}) conditional(s32[]{:T(128)} %convert_element_type.24, () %tuple.48, (f32[1280,1280]{1,0:T(8,128)}, f32[1280,512]{1,0:T(8,128)}) %tuple.49), branch_computations={%region_7.0_spmd, %region_8.0_spmd} | conditional | flops 10066329600 | bytes 11796488 | solution.py:42
  189.0 13.4 %convolution_bitcast_fusion.2 = f32[1,1280,512]{2,1,0:T(8,128)S(1)} fusion(f32[1280,1280]{1,0:T(8,128)} %get-tuple-element.64, f32[1280,512]{1,0:T(8,128)} %get-tuple-element.65), kind=kOutput, calls=%fused_computation.2 | convolution fusion | flops 10066329600 | bytes 11796480 | tf_op jit(solution)/shard_map/cond/branch_1_fun/dot_general | solution.py:37
  202.4 3.9 fusion
  206.3 8.0 %copy.9 = f32[2,8,3,80,512]{4,3,2,1,0:T(8,128)} copy(f32[2,8,3,80,512]{4,3,0,1,2:T(8,128)} %bitcast.45) | data formatting | bytes 15728640 | tf_op jit(solution)/shard_map/transpose | solution.py:23
  214.6 20.3 %reduce-scatter.3.cloned.1.call-done = f32[8,3,80,512]{3,2,1,0:T(8,128)} async-done(((f32[16,3,80,512]{3,2,1,0:T(8,128)}), f32[8,3,80,512]{3,2,1,0:T(8,128)}) %reduce-scatter.3.cloned.1.call-update) | async-done | bytes 3932176 | tf_op jit(solution)/shard_map/reduce_scatter | solution.py:24
  235.0 91.7 %reduce-scatter.5.cloned.1.call-done = f32[1,3,80,512]{3,2,1,0:T(8,128)} async-done(((f32[8,3,80,512]{3,2,1,0:T(8,128)}), f32[1,3,80,512]{3,2,1,0:T(8,128)}) %reduce-scatter.5.cloned.1.call-update) | async-done | bytes 491536 | tf_op jit(solution)/shard_map/reduce_scatter | solution.py:25
  326.7 1.1 fusion.1
  327.9 2.7 fusion.2
  330.6 0.5 copy.16
  331.1 43.8 %all_to_all.10 = f32[16,3,512,32]{2,3,1,0:T(8,128)S(1)} all-to-all(f32[16,3,512,32]{2,3,1,0:T(8,128)S(1)} %bitcast.48), channel_id=1, replica_groups=mesh['prow'=16,'pcol_0'=4,'pcol_1'=2,'pcol_2'=2] {'pcol_0','pcol_1','pco..., dimensions={0} | all-to-all | bytes 6291456 | tf_op jit(solution)/shard_map/all_to_all | solution.py:30
  376.2 19.1 %all_to_all.11 = f32[16,1,3072]{2,1,0:T(1,128)S(1)} all-to-all(f32[16,1,3072]{2,1,0:T(1,128)S(1)} %reshape.130), channel_id=1, replica_groups=mesh['prow'=16,'pcol_0'=4,'pcol_1'=2,'pcol_2'=2] {'prow'}, dimensions={0} | all-to-all | bytes 393216 | tf_op jit(solution)/shard_map/all_to_all | solution.py:30
  395.8 1.1 reduce.6
  397.2 0.6 sub.3
  (21 shorter events, 2.6 us)
Async XLA Ops:
  7.2 135.5 %all-gather.2.cloned.1.call-start = ((), (), s32[]{:S(2)}) async-start(), calls=%async_computation.4 | async-start | bytes 8355840 | tf_op jit(solution)/shard_map/all_gather | solution.py:51
  10.0 224.9 %reduce-scatter.3.cloned.1.call-start = ((), (), s32[]{:S(2)}) async-start(), calls=%async_computation.5 | async-start | bytes 11796480 | tf_op jit(solution)/shard_map/reduce_scatter | solution.py:24
  214.3 113.5 %copy-start = (f32[3,80,512]{2,1,0:T(8,128)S(1)}, f32[3,80,512]{2,1,0:T(8,128)}, u32[]{:S(2)}) copy-start(f32[3,80,512]{2,1,0:T(8,128)} %broadcast_multiply_fusion) | copy-start | bytes 1474564
  214.3 112.4 %reduce-scatter.5.cloned.1.call-start = ((), (), s32[]{:S(2)}) async-start(), calls=%async_computation.6 | async-start | bytes 4423680 | tf_op jit(solution)/shard_map/reduce_scatter | solution.py:25
  327.8 2.7 copy-start.1
  375.4 21.8 %copy-start.2 = (f32[3,32,32]{2,1,0:T(8,128)S(1)}, f32[3,32,32]{2,1,0:T(8,128)}, u32[]{:S(2)}) copy-start(f32[3,32,32]{2,1,0:T(8,128)} %param.19) | copy-start | bytes 36868
Sparse Core Ops, SparseCore 0:
  11.1 131.4 all-gather.1
  214.5 20.4 reduce-scatter.2
  237.5 89.1 reduce-scatter.4
where the time goes:
time: 405 us; the launch traced here: 404 us
  waiting for transfers between devices  245 us (60%)
  blocking collectives  62.9 us (16%)
  matrix products  42.9 us (11%)
  local copies, waits for them, and re-layouts  22.8 us (6%)
  between operations  15.8 us (4%)
  other arithmetic  14.7 us (4%)
    all_gather x1, waiting for transfers between devices, on_device(): piece = lax.all_gather(masked, 'prow', axis=1, tiled=True)  133 us
    reduce_scatter x1, waiting for transfers between devices, sum_by_chip(): return lax.psum_scatter(tiles, chips, scatter_dimension=0, tiled=True)[0]  91.7 us
    all_to_all x2, blocking collectives, sent_and_summed(): tiles = lax.all_to_all(split_up(value, dim, peers), axis, 0, 0, tiled=True)  62.9 us
    dot_general x3, matrix products, dense_product(): return jnp.dot(columns, piece, precision=lax.Precision.HIGHEST)  40.2 us
    reduce_scatter x1, waiting for transfers between devices, sum_by_chip(): tiles = lax.psum_scatter(tiles, core, scatter_dimension=0, tiled=True)  20.3 us
  transfers between devices with their start and end apart: 3, of which 3 were waited for; matrix products, arithmetic and copies ran while one was open for 0% of the time, Pallas kernels for 0%

commit v1 on v0

v1 whole, which is shorter than its diff:
```python
import functools

import jax
import jax.numpy as jnp
from jax import lax
from jax.experimental import pallas as pl
from jax.experimental.pallas import tpu as pltpu
from jax.sharding import Mesh
from jax.sharding import PartitionSpec as P

F32, BF16 = jnp.float32, jnp.bfloat16
NSUP, S, BLK = 3, 512, 8
NZ, NX = 8, 4
ROWS = 80
HALF = 256
UNITS = 2 * NSUP
PIECE = S // 16
PROW = ("y_hi", "z")
PCOL = ("x", "y_lo", "core")


def remote(src, dst, send, recv, sems, device):
    return pltpu.make_async_remote_copy(
        src_ref=src,
        dst_ref=dst,
        send_sem=send.at[sems],
        recv_sem=recv.at[sems],
        device_id=device,
        device_id_type=pl.DeviceIdType.MESH,
    )


def split_bf16(value):
    high = value.astype(BF16)
    return high, (value - high.astype(F32)).astype(BF16)


def kernel(
    anc, a_hbm, panels, dinv, u_out, diag_out,
    a_f32, a_hl, gath, b_hi, b_lo, part, csum, xone, xtwo, ybuf,
    dpart, dsum, dxone, dxtwo, dybuf, dtot, wsend, wrecv,
    a_sem, ys, yr, zs, zr, cs, cr, x1s, x1r, x2s, x2r, es, er,
    dcs, dcr, dx1s, dx1r, dx2s, dx2r, des, der, ws, wr,
):
    yh, z = lax.axis_index("y_hi"), lax.axis_index("z")
    x, yl, core = lax.axis_index("x"), lax.axis_index("y_lo"), lax.axis_index("core")
    own = yh * NZ + z
    z_up, z_dn = lax.rem(z + 1, NZ), lax.rem(z + NZ - 1, NZ)
    x_up, x_dn, x_far = lax.rem(x + 1, NX), lax.rem(x + 3, NX), lax.rem(x + 2, NX)
    to_z = ({"z": z_up}, {"z": z_dn})
    to_x = ({"x": x_up}, {"x": x_dn})
    to_y, to_e, to_core = {"y_hi": 1 - yh}, {"y_lo": 1 - yl}, {"core": 1 - core}

    a_copies = [
        pltpu.make_async_copy(
            a_hbm.at[pl.ds(320 * j, 320)], a_f32.at[pl.ds(320 * j, 320)], a_sem.at[j]
        )
        for j in range(NX)
    ]
    for copy in a_copies:
        copy.start()

    barrier = pltpu.get_barrier_semaphore()
    for device in (*to_z, *to_x, to_y, to_e, to_core):
        pl.semaphore_signal(barrier, inc=1, device_id=device, device_id_type=pl.DeviceIdType.MESH)
    for u in range(UNITS):
        s, h = divmod(u, 2)
        for b in range(ROWS // BLK):
            flag = anc[s, b].astype(F32)
            rows = pl.ds(b * BLK, BLK)
            gath[u, own, rows, :] = panels[s, rows, pl.ds(h * HALF, HALF)] * flag
    pl.semaphore_wait(barrier, 7)

    def ycopy(u, block):
        return remote(gath.at[u, block], gath.at[u, block], ys, yr, (u,), to_y)

    def zcopy(u, d, q, t, back):
        gone = t + 1 if back else t
        origin = lax.rem(z + (NZ - gone if d == 0 else gone), NZ)
        side = yh if q == 0 else 1 - yh
        block = gath.at[u, side * NZ + origin]
        return remote(block, block, zs, zr, (u, d, q, t), to_z[d])

    def arrived(u, q, t):
        dirs = (0, 1) if t < 3 else (q,)
        for d in dirs:
            zcopy(u, d, q, t, True).wait_recv()

    def send_on(u, q, t):
        dirs = (0, 1) if t < 3 else (q,)
        for d in dirs:
            zcopy(u, d, q, t, False).start()

    def first_own(u):
        send_on(u, 0, 0)

    def first_other(u):
        ycopy(u, (1 - yh) * NZ + z).wait_recv()
        send_on(u, 1, 0)

    ycopy(0, own).start()
    first_own(0)
    for u in range(1, UNITS):
        ycopy(u, own).start()
    first_other(0)

    def core_part(u, j):
        return remote(part.at[u, j, :, 1 - core], csum.at[u, j], cs, cr, (u, j), to_core)

    def product(u, j):
        both = jnp.dot(a_hl[j], b_hi[...], preferred_element_type=F32)
        low = jnp.dot(a_hl[j, pl.ds(0, 320)], b_lo[...], preferred_element_type=F32)
        total = both[:320] + (both[320:] + low)
        part[u, j] = total.reshape(2, 2, ROWS, HALF)
        core_part(u, j).start()

    def x_one(v, d, c, one, sems):
        return remote(c.at[v, x_far, d], one.at[v, d], *sems, (v, d), to_x[d])

    def x_two(v, d, c, two, sems):
        return remote(c.at[v, (x_up, x_dn)[d]], two.at[v, d], *sems, (v, d), to_x[d])

    def y_last(v, c, y, sems):
        return remote(c.at[v, x, 1 - yl], y.at[v], *sems, (v,), to_e)

    def sum_stage(j, v, p, c, one, two, y, s1, s2, s3):
        if j == 0:
            for k in range(NX):
                c[v, k] = c[v, k] + p[v, k, :, core]
            for d in range(2):
                x_one(v, d, c, one, s1).start()
        elif j == 1:
            for d in range(2):
                x_one(v, d, c, one, s1).wait_recv()
                to = (x_up, x_dn)[d]
                c[v, to, d] = c[v, to, d] + one[v, d]
                x_two(v, d, c, two, s2).start()
        elif j == 2:
            for d in range(2):
                x_two(v, d, c, two, s2).wait_recv()
            c[v, x] = c[v, x] + two[v, 0] + two[v, 1]
            y_last(v, c, y, s3).start()
        else:
            y_last(v, c, y, s3).wait_recv()
            return c[v, x, yl] + y[v]

    u_args = (part, csum, xone, xtwo, ybuf, (x1s, x1r), (x2s, x2r), (es, er))
    d_args = (dpart, dsum, dxone, dxtwo, dybuf, (dx1s, dx1r), (dx2s, dx2r), (des, der))

    def core_diag(s):
        return remote(dpart.at[s, :, :, 1 - core], dsum.at[s], dcs, dcr, (s,), to_core)

    def local_diag(s):
        mine = jnp.concatenate([gath[2 * s, own], gath[2 * s + 1, own]], axis=1)
        m_hi, m_lo = split_bf16(mine)
        u_t = u_out[s].T
        u_hi, u_lo = split_bf16(u_t)
        terms = jnp.dot(u_lo, m_hi, preferred_element_type=F32)
        terms = terms + jnp.dot(u_hi, m_lo, preferred_element_type=F32)
        terms = terms + jnp.dot(u_hi, m_hi, preferred_element_type=F32)
        dpart[s] = terms.reshape(NX, 2, 2, PIECE, S)
        core_diag(s).start()

    def tick(i, carry):
        for j in range(4):

            @pl.when(i < UNITS)
            def _():
                for q in range(2):
                    if j < 3:
                        arrived(i, q, j)
                        send_on(i, q, j + 1)
                    else:
                        arrived(i, q, 3)

            @pl.when(i + 1 < UNITS)
            def _():
                if j == 0:
                    first_own(i + 1)
                elif j == 1:
                    first_other(i + 1)

            @pl.when(i == 0)
            def _():
                a_copies[j].wait()
                high, low = split_bf16(a_f32[pl.ds(320 * j, 320)])
                a_hl[j, pl.ds(0, 320)] = high
                a_hl[j, pl.ds(320, 320)] = low

            @pl.when((i >= 1) & (i <= UNITS))
            def _():
                if j == 0:
                    for k in range(4):
                        high, low = split_bf16(gath[i - 1, pl.ds(4 * k, 4)].reshape(320, HALF))
                        b_hi[pl.ds(320 * k, 320)] = high
                        b_lo[pl.ds(320 * k, 320)] = low
                product(i - 1, j)

            @pl.when((i >= 2) & (i <= UNITS + 1))
            def _():
                v = i - 2
                if j == 0:
                    for k in range(NX):
                        core_part(v, k).wait_recv()
                final = sum_stage(j, v, *u_args)
                if j == 3:
                    s, h = v // 2, lax.rem(v, 2)
                    columns = pl.ds(pl.multiple_of(h * HALF, HALF), HALF)
                    for b in range(ROWS // BLK):
                        flag = anc[s, b].astype(F32)
                        rows = pl.ds(b * BLK, BLK)
                        u_out[s, rows, columns] = -(final[b * BLK : (b + 1) * BLK] * flag)

            @pl.when((i >= 4) & (lax.rem(i, 2) == 0))
            def _():
                s = i // 2 - 2
                if j == 0:
                    core_diag(s).wait_recv()
                final = sum_stage(j, s, *d_args)
                if j == 3:
                    dtot[s] = final

        @pl.when((i >= 3) & (lax.rem(i, 2) == 1))
        def _():
            local_diag((i - 3) // 2)

        return carry

    lax.fori_loop(0, UNITS + 3, tick, 0)

    group = lax.broadcasted_iota(jnp.int32, (PIECE, 128), 1) // PIECE
    for a in range(4):
        tiles = [dtot[s, :, pl.ds(128 * a, 128)] for s in range(NSUP)]
        for b in range(4):
            block = jnp.zeros((PIECE, 128), F32)
            for s in range(NSUP):
                moved = tiles[s] if s == b else pltpu.roll(tiles[s], (s - b) % 4 * PIECE, 1)
                block = jnp.where(group == s, moved, block)
            wsend[4 * a + b] = block

    def to_owner(d):
        peer = lax.rem(own + d, 16)
        device = {"y_hi": peer // NZ, "z": lax.rem(peer, NZ)}
        return remote(wsend.at[peer], wrecv.at[d], ws, wr, (d,), device)

    for d in range(1, 16):
        to_owner(d).start()
    total = wsend[own]
    for d in range(1, 16):
        to_owner(d).wait_recv()
        total = total + wrecv[d]
    turned = total.T
    for s in range(NSUP):
        diag_out[s] = dinv[s] - turned[s * PIECE : (s + 1) * PIECE]

    for d in range(1, 16):
        to_owner(d).wait_send()

    def drain(u, carry):
        ycopy(u, own).wait_send()
        for t in range(4):
            for q in range(2):
                for d in (0, 1) if t < 3 else (q,):
                    zcopy(u, d, q, t, False).wait_send()
        for j in range(NX):
            core_part(u, j).wait_send()
        for d in range(2):
            x_one(u, d, csum, xone, (x1s, x1r)).wait_send()
            x_two(u, d, csum, xtwo, (x2s, x2r)).wait_send()
        y_last(u, csum, ybuf, (es, er)).wait_send()

        @pl.when(u < NSUP)
        def _():
            core_diag(u).wait_send()
            for d in range(2):
                x_one(u, d, dsum, dxone, (dx1s, dx1r)).wait_send()
                x_two(u, d, dsum, dxtwo, (dx2s, dx2r)).wait_send()
            y_last(u, dsum, dybuf, (des, der)).wait_send()

        return carry

    lax.fori_loop(0, UNITS, drain, 0)


def on_device(ainv, panels, ancestors, dinv):
    dma = pltpu.SemaphoreType.DMA
    vmem = pltpu.VMEM
    whole = pl.BlockSpec(memory_space=pltpu.VMEM)
    pairs = [(UNITS,), (UNITS, 2, 2, 4), (UNITS, NX), (UNITS, 2), (UNITS, 2), (UNITS,)]
    pairs += [(NSUP,), (NSUP, 2), (NSUP, 2), (NSUP,), (16,)]
    return pl.pallas_call(
        kernel,
        out_shape=(
            jax.ShapeDtypeStruct((NSUP, ROWS, S), F32),
            jax.ShapeDtypeStruct((NSUP, PIECE, PIECE), F32),
        ),
        in_specs=[
            pl.BlockSpec(memory_space=pltpu.SMEM),
            pl.BlockSpec(memory_space=pl.ANY),
            whole,
            whole,
        ],
        out_specs=(whole, whole),
        scratch_shapes=[
            vmem((1280, 1280), F32),
            vmem((NX, 640, 1280), BF16),
            vmem((UNITS, 16, ROWS, HALF), F32),
            vmem((1280, HALF), BF16),
            vmem((1280, HALF), BF16),
            vmem((UNITS, NX, 2, 2, ROWS, HALF), F32),
            vmem((UNITS, NX, 2, ROWS, HALF), F32),
            vmem((UNITS, 2, ROWS, HALF), F32),
            vmem((UNITS, 2, 2, ROWS, HALF), F32),
            vmem((UNITS, ROWS, HALF), F32),
            vmem((NSUP, NX, 2, 2, PIECE, S), F32),
            vmem((NSUP, NX, 2, PIECE, S), F32),
            vmem((NSUP, 2, PIECE, S), F32),
            vmem((NSUP, 2, 2, PIECE, S), F32),
            vmem((NSUP, PIECE, S), F32),
            vmem((NSUP, PIECE, S), F32),
            vmem((16, PIECE, 128), F32),
            vmem((16, PIECE, 128), F32),
            dma((NX,)),
            *[dma(shape) for shape in pairs for _ in range(2)],
        ],
        compiler_params=pltpu.CompilerParams(
            collective_id=0, has_side_effects=True, vmem_limit_bytes=60 * 1024 * 1024
        ),
        name="selected_inversion",
    )(ancestors, ainv, panels, dinv)


def solution(mesh):
    split = Mesh(mesh.devices.reshape(2, NZ, NX, 2, 2), PROW + PCOL)
    everywhere = PROW + PCOL
    in_specs = (
        P(PROW, PCOL),
        P(None, everywhere, None),
        P(None, everywhere),
        P(None, PROW, PCOL),
    )
    out_specs = (P(None, everywhere, None), P(None, PROW, PCOL))
    return jax.shard_map(
        on_device, mesh=split, in_specs=in_specs, out_specs=out_specs, check_vma=False
    )
```

time: 405 us -> 173 us (0.43)
  waiting for transfers between devices: 245 us -> 0 us
  Pallas kernels: 0 us -> 167 us
  blocking collectives: 62.9 us -> 0 us
  matrix products: 42.9 us -> 0 us
  local copies, waits for them, and re-layouts: 22.8 us -> 3.26 us
  between operations: 15.8 us -> 0.64 us
  other arithmetic: 14.7 us -> 0 us
    pallas_call x0 -> x1, Pallas kernels: none -> 167 us  [on_device(): pl.pallas_call(kernel, out_shape=(jax.ShapeDtypeStruct((NSUP, ROWS, S), F...]
    all_gather x1 -> x0, waiting for transfers between devices: 133 us -> none  [on_device(): piece = lax.all_gather(masked, 'prow', axis=1, tiled=True)]
    reduce_scatter x2 -> x0, waiting for transfers between devices: 112 us -> none  [the longest x1 91.7 us: sum_by_chip(): return lax.psum_scatter(tiles, chips, scatter_dimension=0, tiled=True)[0]]
    all_to_all x2 -> x0, blocking collectives: 62.9 us -> none  [sent_and_summed(): tiles = lax.all_to_all(split_up(value, dim, peers), axis, 0, 0, tiled=True)]
    dot_general x4 -> x0, matrix products: 42.9 us -> none  [the longest x3 40.2 us: dense_product(): return jnp.dot(columns, piece, precision=lax.Precision.HIGHEST)]
    transpose x1 -> x0, local copies, waits for them, and re-layouts: 8.01 us -> none  [sum_by_chip(): tiles = tiles.reshape(*sizes, *inside).swapaxes(0, 1).reshape(-1, *inside)]
    squeeze x1 -> x0, local copies, waits for them, and re-layouts: 6.65 us -> none  [on_device(): total = total.at[member].add(apply_rows(ainv, piece[member]))]
    scatter-add x2 -> x0, local copies, waits for them, and re-layouts: 5.76 us -> none  [on_device(): total = total.at[member].add(apply_rows(ainv, piece[member]))]
  transfers between devices with their start and end apart: 3 -> 0, of which waited for: 3 -> 0; matrix products, arithmetic and copies ran while one was open for 0% -> 0% of each run, Pallas kernels for 0% -> 0%
where the time goes in v1:
time: 173 us; the launch traced here: 171 us
  Pallas kernels  167 us (97%)
  local copies, waits for them, and re-layouts  3.26 us (2%)
    pallas_call x1, Pallas kernels, on_device(): pl.pallas_call(kernel, out_shape=(jax.ShapeDtypeStruct((NSUP, ROWS, S), F...  167 us

profile of v1, /device:TPU:32, one launch (start us, length us, event | category | flops | bytes accessed | tf_op | source)
XLA Modules:
  0.0 171.4 jit_solution(9821592202766828229)
XLA Ops:
  0.6 167.5 %selected_inversion.1 = (f32[3,80,512]{2,1,0:T(8,128)}, f32[3,32,32]{2,1,0:T(8,128)}) custom-call(s32[3,10]{1,0:T(4,128)} %anc.1, f32[1280,1280]{1,0:T(8,128)} %a_hbm.1, f32[3,80,512]{2,1,0:T(8,128)} %panels.1, f32[3,32,32]{2,1,0:T(8,128)} %dinv.1), custom_call_target="tpu_custom_call" | custom-call | tf_op jit(solution)/shard_map/selected_inversion/pallas_call | solution.py:291
  168.1 1.8 %copy.8 = f32[3,80,512]{2,1,0:T(8,128)} copy(f32[3,80,512]{2,1,0:T(8,128)} %get-tuple-element.4) | data formatting | bytes 983040
  169.9 1.4 copy.9

commit v2 on v1

v2 whole, which is shorter than its diff:
```python
import functools

import jax
import jax.numpy as jnp
from jax import lax
from jax.experimental import pallas as pl
from jax.experimental.pallas import tpu as pltpu
from jax.sharding import Mesh
from jax.sharding import PartitionSpec as P

F32, BF16 = jnp.float32, jnp.bfloat16
NSUP, S, BLK = 3, 512, 8
NZ, NX = 8, 4
ROWS = 80
HALF = 256
UNITS = 2 * NSUP
PIECE = S // 16
CROSS = 32
PROW = ("y_hi", "z")
PCOL = ("x", "y_lo", "core")


def remote(src, dst, send, recv, sems, device):
    return pltpu.make_async_remote_copy(
        src_ref=src,
        dst_ref=dst,
        send_sem=send.at[sems],
        recv_sem=recv.at[sems],
        device_id=device,
        device_id_type=pl.DeviceIdType.MESH,
    )


def split_bf16(value):
    high = value.astype(BF16)
    return high, (value - high.astype(F32)).astype(BF16)


def kernel(
    anc, a_hbm, panels, dinv, u_out, diag_out,
    a_f32, a_hl, gath, b_hi, b_lo, part, csum, xone, xtwo, ybuf,
    dpart, dsum, dxone, dxtwo, dybuf, wsend, wrecv, rows_all, mt_hi, mt_lo,
    a_sem, ys, yr, fs, fr, zs, zr, cs, cr, x1s, x1r, x2s, x2r, es, er,
    dcs, dcr, dx1s, dx1r, dx2s, dx2r, des, der, ws, wr, gs, gr,
):
    yh, z = lax.axis_index("y_hi"), lax.axis_index("z")
    x, yl, core = lax.axis_index("x"), lax.axis_index("y_lo"), lax.axis_index("core")
    own = yh * NZ + z
    z_up, z_dn = lax.rem(z + 1, NZ), lax.rem(z + NZ - 1, NZ)
    x_up, x_dn, x_far = lax.rem(x + 1, NX), lax.rem(x + 3, NX), lax.rem(x + 2, NX)
    to_z = ({"z": z_up}, {"z": z_dn})
    to_x = ({"x": x_up}, {"x": x_dn})
    to_y, to_e, to_core = {"y_hi": 1 - yh}, {"y_lo": 1 - yl}, {"core": 1 - core}

    a_copies = [
        pltpu.make_async_copy(
            a_hbm.at[pl.ds(320 * j, 320)], a_f32.at[pl.ds(320 * j, 320)], a_sem.at[j]
        )
        for j in range(NX)
    ]
    for copy in a_copies:
        copy.start()

    barrier = pltpu.get_barrier_semaphore()
    for device in (*to_z, *to_x, to_y, to_e, to_core):
        pl.semaphore_signal(barrier, inc=1, device_id=device, device_id_type=pl.DeviceIdType.MESH)

    def mask_panels(s):
        for b in range(ROWS // BLK):
            flag = anc[s, b].astype(F32)
            rows = pl.ds(b * BLK, BLK)
            masked = panels[s, rows, :] * flag
            for h in range(2):
                gath[2 * s + h, own, rows, :] = masked[:, h * HALF : (h + 1) * HALF]
            if s > 0:
                rows_all[s - 1, x, yl, core, rows, :] = masked

    for s in range(NSUP):
        mask_panels(s)
    pl.semaphore_wait(barrier, 7)

    def origin_of(d, gone):
        return lax.rem(z + (NZ - gone if d == 0 else gone), NZ)

    def ycopy(u, block):
        return remote(gath.at[u, block], gath.at[u, block], ys, yr, (u,), to_y)

    def zcopy(u, d, q, t, back):
        side = yh if q == 0 else 1 - yh
        low, high = (0, ROWS) if q == 0 else (CROSS, ROWS)
        if t == 3:
            middle = (low + high) // 2
            low, high = (low, middle) if d == 0 else (middle, high)
        origin = origin_of(d, t + 1 if back else t)
        block = gath.at[u, side * NZ + origin, pl.ds(low, high - low)]
        return remote(block, block, zs, zr, (u, d, q, t), to_z[d])

    def across(u, k, back):
        d, t = divmod(k, 3)
        origin = origin_of(0, 4) if k == 6 else origin_of(d, t + 1)
        side = 1 - yh if back else yh
        block = gath.at[u, side * NZ + origin, pl.ds(0, CROSS)]
        return remote(block, block, fs, fr, (u, k), to_y)

    def pass_on(u, t):
        for q in range(2):
            for d in range(2):
                zcopy(u, d, q, t, True).wait_recv()
                zcopy(u, d, q, t + 1, False).start()
                if q == 0:
                    across(u, 3 * d + t, False).start()

    def first_own(u):
        for d in range(2):
            zcopy(u, d, 0, 0, False).start()

    def first_other(u):
        ycopy(u, (1 - yh) * NZ + z).wait_recv()
        for d in range(2):
            zcopy(u, d, 1, 0, False).start()

    def last_across(u):
        zcopy(u, 0, 0, 3, True).wait_recv()
        across(u, 6, False).start()

    def gathered(u):
        zcopy(u, 1, 0, 3, True).wait_recv()
        for d in range(2):
            zcopy(u, d, 1, 3, True).wait_recv()
        for k in range(7):
            across(u, k, True).wait_recv()

    first_own(0)
    for u in range(UNITS):
        ycopy(u, own).start()
    first_own(1)
    first_other(0)

    mine = rows_all.at[:, x, yl, core]

    def rows_y():
        return remote(mine, mine, gs, gr, (0,), to_e)

    def rows_x(d, step):
        if step == 0:
            block = rows_all.at[:, x, :, core]
        else:
            block = rows_all.at[:, (x_dn, x_up)[d], d, core]
        return remote(block, block, gs, gr, (1 + 2 * step + d,), to_x[d])

    def rows_core():
        block = rows_all.at[:, :, :, core]
        return remote(block, block, gs, gr, (5,), to_core)

    rows_y().start()

    def core_part(u, j):
        return remote(part.at[u, j, :, 1 - core], csum.at[u, j], cs, cr, (u, j), to_core)

    def product(u, j):
        both = jnp.dot(a_hl[j], b_hi[...], preferred_element_type=F32)
        low = jnp.dot(a_hl[j, pl.ds(0, 320)], b_lo[...], preferred_element_type=F32)
        total = both[:320] + (both[320:] + low)
        part[u, j] = total.reshape(2, 2, ROWS, HALF)
        core_part(u, j).start()

    def x_one(v, d, c, one, sems):
        return remote(c.at[v, x_far, d], one.at[v, d], *sems, (v, d), to_x[d])

    def x_two(v, d, c, two, sems):
        return remote(c.at[v, (x_up, x_dn)[d]], two.at[v, d], *sems, (v, d), to_x[d])

    def y_last(v, c, y, sems):
        return remote(c.at[v, x, 1 - yl], y.at[v], *sems, (v,), to_e)

    def sum_stage(j, v, p, c, one, two, y, s1, s2, s3):
        if j == 0:
            c[v, x_far] = c[v, x_far] + p[v, x_far, :, core]
            for d in range(2):
                x_one(v, d, c, one, s1).start()
            for k in (x_up, x_dn, x):
                c[v, k] = c[v, k] + p[v, k, :, core]
        elif j == 1:
            for d in range(2):
                x_one(v, d, c, one, s1).wait_recv()
                to = (x_up, x_dn)[d]
                c[v, to, d] = c[v, to, d] + one[v, d]
                x_two(v, d, c, two, s2).start()
        elif j == 2:
            for d in range(2):
                x_two(v, d, c, two, s2).wait_recv()
            c[v, x, 1 - yl] = c[v, x, 1 - yl] + two[v, 0, 1 - yl] + two[v, 1, 1 - yl]
            y_last(v, c, y, s3).start()
            c[v, x, yl] = c[v, x, yl] + two[v, 0, yl] + two[v, 1, yl]
        else:
            y_last(v, c, y, s3).wait_recv()
            return c[v, x, yl] + y[v]

    u_args = (part, csum, xone, xtwo, ybuf, (x1s, x1r), (x2s, x2r), (es, er))
    d_args = (dpart, dsum, dxone, dxtwo, dybuf, (dx1s, dx1r), (dx2s, dx2r), (des, der))

    def sum_unit(j, v):
        if j == 0:
            for k in range(NX):
                core_part(v, k).wait_recv()
        final = sum_stage(j, v, *u_args)
        if j == 3:
            s, h = v // 2, v % 2
            columns = pl.ds(h * HALF, HALF) if isinstance(v, int) else pl.ds(pl.multiple_of(h * HALF, HALF), HALF)
            for b in range(ROWS // BLK):
                flag = anc[s, b].astype(F32)
                rows = pl.ds(b * BLK, BLK)
                u_out[s, rows, columns] = -(final[b * BLK : (b + 1) * BLK] * flag)

    def core_diag(s):
        return remote(dpart.at[s, :, :, 1 - core], dsum.at[s], dcs, dcr, (s,), to_core)

    def local_diag(s):
        own_rows = jnp.concatenate([gath[2 * s, own], gath[2 * s + 1, own]], axis=1)
        m_hi, m_lo = split_bf16(own_rows)
        u_hi, u_lo = split_bf16(u_out[s].T)
        terms = jnp.dot(u_lo, m_hi, preferred_element_type=F32)
        terms = terms + jnp.dot(u_hi, m_lo, preferred_element_type=F32)
        terms = terms + jnp.dot(u_hi, m_hi, preferred_element_type=F32)
        dpart[s] = terms.reshape(NX, 2, 2, PIECE, S)
        core_diag(s).start()

    def turn_rows(s):
        for k in range(10):
            piece = rows_all[s - 1].reshape(1280, S)[128 * k : 128 * (k + 1)]
            high, low = split_bf16(piece.T)
            mt_hi[s - 1, :, pl.ds(128 * k, 128)] = high
            mt_lo[s - 1, :, pl.ds(128 * k, 128)] = low

    def half_diag(s, h):
        for k in range(4):
            high, low = split_bf16(part[2 * s + h, k].reshape(320, HALF))
            b_hi[pl.ds(320 * k, 320)] = high
            b_lo[pl.ds(320 * k, 320)] = low
        terms = jnp.dot(mt_lo[s - 1], b_hi[...], preferred_element_type=F32)
        terms = terms + jnp.dot(mt_hi[s - 1], b_lo[...], preferred_element_type=F32)
        terms = terms + jnp.dot(mt_hi[s - 1], b_hi[...], preferred_element_type=F32)
        dpart[s, pl.ds(2 * h, 2)] = (-terms.T).reshape(2, 2, 2, PIECE, S)

    group = lax.broadcasted_iota(jnp.int32, (BLK, 128), 1) // PIECE

    def to_owner(s, d):
        peer = lax.rem(own + d, 16)
        device = {"y_hi": peer // NZ, "z": lax.rem(peer, NZ)}
        return remote(wsend.at[s, peer], wrecv.at[s, d], ws, wr, (s, d), device)

    def send_to_owners(s, total):
        for a in range(4):
            for b in range(4):
                block = jnp.zeros((BLK, 128), F32)
                for k in range(4):
                    tile = total[k * BLK : (k + 1) * BLK, 128 * a : 128 * (a + 1)]
                    moved = tile if k == b else pltpu.roll(tile, (k - b) % 4 * PIECE, 1)
                    block = jnp.where(group == k, moved, block)
                wsend[s, 4 * a + b] = block
        for d in range(1, 16):
            to_owner(s, d).start()

    def sum_diag(j, s):
        if j == 0:
            core_diag(s).wait_recv()
        final = sum_stage(j, s, *d_args)
        if j == 3:
            send_to_owners(s, final)

    def at(condition):
        return pl.when(condition)

    def alive(u):
        return (u >= 0) & (u < UNITS)

    def tick(k, carry):
        multiplies = alive(k - 5)

        @at(alive(k - 4))
        def _():
            last_across(k - 4)

        @at(alive(k - 3))
        def _():
            pass_on(k - 3, 2)

        @at(k < UNITS)
        def _():
            first_other(k)

        @at(alive(k - 8))
        def _():
            sum_unit(3, k - 8)

        @at(k == 10)
        def _():
            sum_diag(1, 1)
            sum_diag(1, 0)

        @at(multiplies)
        def _():
            gathered(k - 5)
            for c in range(4):
                high, low = split_bf16(gath[k - 5, pl.ds(4 * c, 4)].reshape(320, HALF))
                b_hi[pl.ds(320 * c, 320)] = high
                b_lo[pl.ds(320 * c, 320)] = low
            product(k - 5, 0)

        @at(alive(k - 2))
        def _():
            pass_on(k - 2, 1)

        @at(k + 1 < UNITS)
        def _():
            first_own(k + 1)

        @at(alive(k - 6))
        def _():
            sum_unit(0, k - 6)

        @at(multiplies)
        def _():
            product(k - 5, 1)

        @at(alive(k - 1))
        def _():
            pass_on(k - 1, 0)

        @at(k <= NX)
        def _():
            rows = pl.ds(pl.multiple_of((k - 1) * 320, 320), 320)
            pltpu.make_async_copy(a_hbm.at[rows], a_f32.at[rows], a_sem.at[k - 1]).wait()
            high, low = split_bf16(a_f32[rows])
            a_hl[k - 1, pl.ds(0, 320)] = high
            a_hl[k - 1, pl.ds(320, 320)] = low

        @at(multiplies)
        def _():
            product(k - 5, 2)

        @at(alive(k - 7))
        def _():
            sum_unit(2, k - 7)

        @at(k == 10)
        def _():
            half_diag(2, 0)
            sum_diag(2, 1)
            sum_diag(2, 0)
            for c in range(4):
                high, low = split_bf16(gath[5, pl.ds(4 * c, 4)].reshape(320, HALF))
                b_hi[pl.ds(320 * c, 320)] = high
                b_lo[pl.ds(320 * c, 320)] = low

        @at(multiplies)
        def _():
            product(k - 5, 3)

        @at(alive(k - 6))
        def _():
            sum_unit(1, k - 6)

        @at(k == 6)
        def _():
            rows_core().wait_recv()
            turn_rows(1)

        @at(k == 7)
        def _():
            turn_rows(2)

        @at(k == 8)
        def _():
            half_diag(1, 0)

        @at(k == 9)
        def _():
            half_diag(1, 1)
            core_diag(1).start()
            local_diag(0)
            sum_diag(0, 1)
            sum_diag(0, 0)

        @at(k == 1)
        def _():
            rows_y().wait_recv()
            for d in range(2):
                rows_x(d, 0).start()

        @at(k == 3)
        def _():
            for d in range(2):
                rows_x(d, 0).wait_recv()
                rows_x(d, 1).start()

        @at(k == 5)
        def _():
            for d in range(2):
                rows_x(d, 1).wait_recv()
            rows_core().start()

        return carry

    lax.fori_loop(1, UNITS + 5, tick, 0)

    half_diag(2, 1)
    core_diag(2).start()
    sum_unit(0, 5)
    sum_diag(0, 2)
    sum_unit(2, 4)
    sum_diag(3, 1)
    sum_diag(3, 0)
    sum_unit(3, 3)
    sum_diag(1, 2)
    sum_unit(1, 5)
    sum_unit(3, 4)
    sum_diag(2, 2)
    sum_unit(2, 5)
    sum_diag(3, 2)
    sum_unit(3, 5)

    for s in range(NSUP):
        total = wsend[s, own]
        for d in range(1, 16):
            to_owner(s, d).wait_recv()
            total = total + wrecv[s, d]
        pieces = [total] + [pltpu.roll(total, 128 - k * PIECE, 1) for k in range(1, 4)]
        turned = jnp.concatenate(pieces, axis=0).T
        diag_out[s] = dinv[s] - turned[:PIECE]

    def drain(u, carry):
        ycopy(u, own).wait_send()
        for k in range(7):
            across(u, k, False).wait_send()
        for t in range(4):
            for q in range(2):
                for d in range(2):
                    zcopy(u, d, q, t, False).wait_send()
        for j in range(NX):
            core_part(u, j).wait_send()
        for d in range(2):
            x_one(u, d, csum, xone, (x1s, x1r)).wait_send()
            x_two(u, d, csum, xtwo, (x2s, x2r)).wait_send()
        y_last(u, csum, ybuf, (es, er)).wait_send()

        @pl.when(u < NSUP)
        def _():
            core_diag(u).wait_send()
            for d in range(2):
                x_one(u, d, dsum, dxone, (dx1s, dx1r)).wait_send()
                x_two(u, d, dsum, dxtwo, (dx2s, dx2r)).wait_send()
            y_last(u, dsum, dybuf, (des, der)).wait_send()
            for d in range(1, 16):
                to_owner(u, d).wait_send()

        return carry

    lax.fori_loop(0, UNITS, drain, 0)
    rows_y().wait_send()
    for d in range(2):
        rows_x(d, 0).wait_send()
        rows_x(d, 1).wait_send()
    rows_core().wait_send()


def on_device(ainv, panels, ancestors, dinv):
    dma = pltpu.SemaphoreType.DMA
    vmem = pltpu.VMEM
    whole = pl.BlockSpec(memory_space=pltpu.VMEM)
    pairs = [(UNITS,), (UNITS, 7), (UNITS, 2, 2, 4), (UNITS, NX), (UNITS, 2), (UNITS, 2)]
    pairs += [(UNITS,), (NSUP,), (NSUP, 2), (NSUP, 2), (NSUP,), (NSUP, 16), (6,)]
    return pl.pallas_call(
        kernel,
        out_shape=(
            jax.ShapeDtypeStruct((NSUP, ROWS, S), F32),
            jax.ShapeDtypeStruct((NSUP, PIECE, PIECE), F32),
        ),
        in_specs=[
            pl.BlockSpec(memory_space=pltpu.SMEM),
            pl.BlockSpec(memory_space=pl.ANY),
            whole,
            whole,
        ],
        out_specs=(whole, whole),
        scratch_shapes=[
            vmem((1280, 1280), F32),
            vmem((NX, 640, 1280), BF16),
            vmem((UNITS, 16, ROWS, HALF), F32),
            vmem((1280, HALF), BF16),
            vmem((1280, HALF), BF16),
            vmem((UNITS, NX, 2, 2, ROWS, HALF), F32),
            vmem((UNITS, NX, 2, ROWS, HALF), F32),
            vmem((UNITS, 2, ROWS, HALF), F32),
            vmem((UNITS, 2, 2, ROWS, HALF), F32),
            vmem((UNITS, ROWS, HALF), F32),
            vmem((NSUP, NX, 2, 2, PIECE, S), F32),
            vmem((NSUP, NX, 2, PIECE, S), F32),
            vmem((NSUP, 2, PIECE, S), F32),
            vmem((NSUP, 2, 2, PIECE, S), F32),
            vmem((NSUP, PIECE, S), F32),
            vmem((NSUP, 16, BLK, 128), F32),
            vmem((NSUP, 16, BLK, 128), F32),
            vmem((2, NX, 2, 2, ROWS, S), F32),
            vmem((2, S, 1280), BF16),
            vmem((2, S, 1280), BF16),
            dma((NX,)),
            *[dma(shape) for shape in pairs for _ in range(2)],
        ],
        compiler_params=pltpu.CompilerParams(
            collective_id=0, has_side_effects=True, vmem_limit_bytes=60 * 1024 * 1024
        ),
        name="selected_inversion",
    )(ancestors, ainv, panels, dinv)


def solution(mesh):
    split = Mesh(mesh.devices.reshape(2, NZ, NX, 2, 2), PROW + PCOL)
    everywhere = PROW + PCOL
    in_specs = (
        P(PROW, PCOL),
        P(None, everywhere, None),
        P(None, everywhere),
        P(None, PROW, PCOL),
    )
    out_specs = (P(None, everywhere, None), P(None, PROW, PCOL))
    return jax.shard_map(
        on_device, mesh=split, in_specs=in_specs, out_specs=out_specs, check_vma=False
    )
```

time: 173 us -> 145 us (0.84)
  Pallas kernels: 167 us -> 140 us
    pallas_call x1, Pallas kernels: 167 us -> 140 us  [on_device(): pl.pallas_call(kernel, out_shape=(jax.ShapeDtypeStruct((NSUP, ROWS, S), F...]
where the time goes in v2:
time: 145 us; the launch traced here: 144 us
  Pallas kernels  140 us (97%)
  local copies, waits for them, and re-layouts  3.26 us (2%)
    pallas_call x1, Pallas kernels, on_device(): pl.pallas_call(kernel, out_shape=(jax.ShapeDtypeStruct((NSUP, ROWS, S), F...  140 us
    unnamed x2, local copies, waits for them, and re-layouts  3.26 us

profile of v2, /device:TPU:32, one launch (start us, length us, event | category | flops | bytes accessed | tf_op | source)
XLA Modules:
  0.0 144.0 jit_solution(1734636075384793890)
XLA Ops:
  0.6 140.1 %selected_inversion.1 = (f32[3,80,512]{2,1,0:T(8,128)}, f32[3,32,32]{2,1,0:T(8,128)}) custom-call(s32[3,10]{1,0:T(4,128)} %anc.1, f32[1280,1280]{1,0:T(8,128)} %a_hbm.1, f32[3,80,512]{2,1,0:T(8,128)} %panels.1, f32[3,32,32]{2,1,0:T(8,128)} %dinv.1), custom_call_target="tpu_custom_call" | custom-call | tf_op jit(solution)/shard_map/selected_inversion/pallas_call | solution.py:473
  140.7 1.8 %copy.8 = f32[3,80,512]{2,1,0:T(8,128)} copy(f32[3,80,512]{2,1,0:T(8,128)} %get-tuple-element.4) | data formatting | bytes 983040
  142.6 1.4 copy.9

commit v3 on v2

--- a/solution.py
+++ b/solution.py
@@ -72,8 +72,8 @@
             masked = panels[s, rows, :] * flag
             for h in range(2):
                 gath[2 * s + h, own, rows, :] = masked[:, h * HALF : (h + 1) * HALF]
-            if s > 0:
-                rows_all[s - 1, x, yl, core, rows, :] = masked
+            if s == 2:
+                rows_all[x, yl, core, rows, :] = masked
 
     for s in range(NSUP):
         mask_panels(s)
@@ -136,32 +136,33 @@
     first_own(1)
     first_other(0)
 
-    mine = rows_all.at[:, x, yl, core]
+    mine = rows_all.at[x, yl, core]
 
     def rows_y():
         return remote(mine, mine, gs, gr, (0,), to_e)
 
     def rows_x(d, step):
         if step == 0:
-            block = rows_all.at[:, x, :, core]
+            block = rows_all.at[x, :, core]
         else:
-            block = rows_all.at[:, (x_dn, x_up)[d], d, core]
+            block = rows_all.at[(x_dn, x_up)[d], d, core]
         return remote(block, block, gs, gr, (1 + 2 * step + d,), to_x[d])
 
     def rows_core():
-        block = rows_all.at[:, :, :, core]
+        block = rows_all.at[:, :, core]
         return remote(block, block, gs, gr, (5,), to_core)
 
     rows_y().start()
 
     def core_part(u, j):
-        return remote(part.at[u, j, :, 1 - core], csum.at[u, j], cs, cr, (u, j), to_core)
+        two = pl.ds(2 * j, 2)
+        return remote(part.at[u, two, :, 1 - core], csum.at[u, two], cs, cr, (u, j), to_core)
 
     def product(u, j):
         both = jnp.dot(a_hl[j], b_hi[...], preferred_element_type=F32)
-        low = jnp.dot(a_hl[j, pl.ds(0, 320)], b_lo[...], preferred_element_type=F32)
-        total = both[:320] + (both[320:] + low)
-        part[u, j] = total.reshape(2, 2, ROWS, HALF)
+        low = jnp.dot(a_hl[j, pl.ds(0, 640)], b_lo[...], preferred_element_type=F32)
+        total = both[:640] + (both[640:] + low)
+        part[u, pl.ds(2 * j, 2)] = total.reshape(2, 2, 2, ROWS, HALF)
         core_part(u, j).start()
 
     def x_one(v, d, c, one, sems):
@@ -201,7 +202,7 @@
 
     def sum_unit(j, v):
         if j == 0:
-            for k in range(NX):
+            for k in range(2):
                 core_part(v, k).wait_recv()
         final = sum_stage(j, v, *u_args)
         if j == 3:
@@ -225,22 +226,22 @@
         dpart[s] = terms.reshape(NX, 2, 2, PIECE, S)
         core_diag(s).start()
 
-    def turn_rows(s):
+    def turn_rows():
         for k in range(10):
-            piece = rows_all[s - 1].reshape(1280, S)[128 * k : 128 * (k + 1)]
+            piece = rows_all[...].reshape(1280, S)[128 * k : 128 * (k + 1)]
             high, low = split_bf16(piece.T)
-            mt_hi[s - 1, :, pl.ds(128 * k, 128)] = high
-            mt_lo[s - 1, :, pl.ds(128 * k, 128)] = low
-
-    def half_diag(s, h):
+            mt_hi[:, pl.ds(128 * k, 128)] = high
+            mt_lo[:, pl.ds(128 * k, 128)] = low
+
+    def half_diag(h):
         for k in range(4):
-            high, low = split_bf16(part[2 * s + h, k].reshape(320, HALF))
+            high, low = split_bf16(part[4 + h, k].reshape(320, HALF))
             b_hi[pl.ds(320 * k, 320)] = high
             b_lo[pl.ds(320 * k, 320)] = low
-        terms = jnp.dot(mt_lo[s - 1], b_hi[...], preferred_element_type=F32)
-        terms = terms + jnp.dot(mt_hi[s - 1], b_lo[...], preferred_element_type=F32)
-        terms = terms + jnp.dot(mt_hi[s - 1], b_hi[...], preferred_element_type=F32)
-        dpart[s, pl.ds(2 * h, 2)] = (-terms.T).reshape(2, 2, 2, PIECE, S)
+        terms = jnp.dot(mt_lo[...], b_hi[...], preferred_element_type=F32)
+        terms = terms + jnp.dot(mt_hi[...], b_lo[...], preferred_element_type=F32)
+        terms = terms + jnp.dot(mt_hi[...], b_hi[...], preferred_element_type=F32)
+        dpart[2, pl.ds(2 * h, 2)] = (-terms.T).reshape(2, 2, 2, PIECE, S)
 
     group = lax.broadcasted_iota(jnp.int32, (BLK, 128), 1) // PIECE
 
@@ -275,9 +276,9 @@
         return (u >= 0) & (u < UNITS)
 
     def tick(k, carry):
-        multiplies = alive(k - 5)
-
-        @at(alive(k - 4))
+        multiplies = alive(k - 4)
+
+        @at(multiplies)
         def _():
             last_across(k - 4)
 
@@ -289,23 +290,19 @@
         def _():
             first_other(k)
 
-        @at(alive(k - 8))
-        def _():
-            sum_unit(3, k - 8)
-
-        @at(k == 10)
-        def _():
-            sum_diag(1, 1)
-            sum_diag(1, 0)
-
-        @at(multiplies)
-        def _():
-            gathered(k - 5)
-            for c in range(4):
-                high, low = split_bf16(gath[k - 5, pl.ds(4 * c, 4)].reshape(320, HALF))
-                b_hi[pl.ds(320 * c, 320)] = high
-                b_lo[pl.ds(320 * c, 320)] = low
-            product(k - 5, 0)
+        @at(alive(k - 6))
+        def _():
+            sum_unit(2, k - 6)
+
+        @at(k == 5)
+        def _():
+            rows_core().wait_recv()
+            turn_rows()
+
+        @at(k == 9)
+        def _():
+            sum_diag(2, 0)
+            half_diag(0)
 
         @at(alive(k - 2))
         def _():
@@ -315,72 +312,59 @@
         def _():
             first_own(k + 1)
 
-        @at(alive(k - 6))
-        def _():
-            sum_unit(0, k - 6)
-
-        @at(multiplies)
-        def _():
-            product(k - 5, 1)
-
-        @at(alive(k - 1))
-        def _():
-            pass_on(k - 1, 0)
+        @at(alive(k - 5))
+        def _():
+            sum_unit(0, k - 5)
+
+        @at(k == 8)
+        def _():
+            sum_diag(0, 0)
 
         @at(k <= NX)
         def _():
             rows = pl.ds(pl.multiple_of((k - 1) * 320, 320), 320)
             pltpu.make_async_copy(a_hbm.at[rows], a_f32.at[rows], a_sem.at[k - 1]).wait()
             high, low = split_bf16(a_f32[rows])
-            a_hl[k - 1, pl.ds(0, 320)] = high
-            a_hl[k - 1, pl.ds(320, 320)] = low
+            half, place = (k - 1) // 2, lax.rem(k - 1, 2) * 320
+            a_hl[half, pl.ds(pl.multiple_of(place, 320), 320)] = high
+            a_hl[half, pl.ds(pl.multiple_of(640 + place, 320), 320)] = low
+
+        @at(alive(k - 6))
+        def _():
+            sum_unit(3, k - 6)
+
+        @at((k == 7) | (k == 9))
+        def _():
+            local_diag((k - 7) // 2)
+
+        @at(k == 9)
+        def _():
+            sum_diag(3, 0)
 
         @at(multiplies)
         def _():
-            product(k - 5, 2)
-
-        @at(alive(k - 7))
-        def _():
-            sum_unit(2, k - 7)
-
-        @at(k == 10)
-        def _():
-            half_diag(2, 0)
-            sum_diag(2, 1)
-            sum_diag(2, 0)
+            gathered(k - 4)
             for c in range(4):
-                high, low = split_bf16(gath[5, pl.ds(4 * c, 4)].reshape(320, HALF))
+                high, low = split_bf16(gath[k - 4, pl.ds(4 * c, 4)].reshape(320, HALF))
                 b_hi[pl.ds(320 * c, 320)] = high
                 b_lo[pl.ds(320 * c, 320)] = low
+            product(k - 4, 0)
+
+        @at(alive(k - 1))
+        def _():
+            pass_on(k - 1, 0)
+
+        @at(alive(k - 5))
+        def _():
+            sum_unit(1, k - 5)
+
+        @at(k == 8)
+        def _():
+            sum_diag(1, 0)
 
         @at(multiplies)
         def _():
-            product(k - 5, 3)
-
-        @at(alive(k - 6))
-        def _():
-            sum_unit(1, k - 6)
-
-        @at(k == 6)
-        def _():
-            rows_core().wait_recv()
-            turn_rows(1)
-
-        @at(k == 7)
-        def _():
-            turn_rows(2)
-
-        @at(k == 8)
-        def _():
-            half_diag(1, 0)
-
-        @at(k == 9)
-        def _():
-            half_diag(1, 1)
-            core_diag(1).start()
-            local_diag(0)
-            sum_diag(0, 1)
-            sum_diag(0, 0)
+            product(k - 4, 1)
 
         @at(k == 1)
         def _():
@@ -388,13 +372,13 @@
             for d in range(2):
                 rows_x(d, 0).start()
 
-        @at(k == 3)
+        @at(k == 2)
         def _():
             for d in range(2):
                 rows_x(d, 0).wait_recv()
                 rows_x(d, 1).start()
 
-        @at(k == 5)
+        @at(k == 3)
         def _():
             for d in range(2):
                 rows_x(d, 1).wait_recv()
@@ -402,19 +386,20 @@
 
         return carry
 
-    lax.fori_loop(1, UNITS + 5, tick, 0)
-
-    half_diag(2, 1)
+    lax.fori_loop(1, UNITS + 4, tick, 0)
+
+    sum_diag(0, 1)
+    sum_unit(0, 5)
+    half_diag(1)
     core_diag(2).start()
-    sum_unit(0, 5)
+    sum_diag(1, 1)
+    sum_unit(2, 4)
     sum_diag(0, 2)
-    sum_unit(2, 4)
+    sum_unit(1, 5)
+    sum_diag(2, 1)
+    sum_unit(3, 4)
+    sum_diag(1, 2)
     sum_diag(3, 1)
-    sum_diag(3, 0)
-    sum_unit(3, 3)
-    sum_diag(1, 2)
-    sum_unit(1, 5)
-    sum_unit(3, 4)
     sum_diag(2, 2)
     sum_unit(2, 5)
     sum_diag(3, 2)
@@ -437,7 +422,7 @@
             for q in range(2):
                 for d in range(2):
                     zcopy(u, d, q, t, False).wait_send()
-        for j in range(NX):
+        for j in range(2):
             core_part(u, j).wait_send()
         for d in range(2):
             x_one(u, d, csum, xone, (x1s, x1r)).wait_send()
@@ -468,7 +453,7 @@
     dma = pltpu.SemaphoreType.DMA
     vmem = pltpu.VMEM
     whole = pl.BlockSpec(memory_space=pltpu.VMEM)
-    pairs = [(UNITS,), (UNITS, 7), (UNITS, 2, 2, 4), (UNITS, NX), (UNITS, 2), (UNITS, 2)]
+    pairs = [(UNITS,), (UNITS, 7), (UNITS, 2, 2, 4), (UNITS, 2), (UNITS, 2), (UNITS, 2)]
     pairs += [(UNITS,), (NSUP,), (NSUP, 2), (NSUP, 2), (NSUP,), (NSUP, 16), (6,)]
     return pl.pallas_call(
         kernel,
@@ -485,7 +470,7 @@
         out_specs=(whole, whole),
         scratch_shapes=[
             vmem((1280, 1280), F32),
-            vmem((NX, 640, 1280), BF16),
+            vmem((2, 1280, 1280), BF16),
             vmem((UNITS, 16, ROWS, HALF), F32),
             vmem((1280, HALF), BF16),
             vmem((1280, HALF), BF16),
@@ -501,9 +486,9 @@
             vmem((NSUP, PIECE, S), F32),
             vmem((NSUP, 16, BLK, 128), F32),
             vmem((NSUP, 16, BLK, 128), F32),
-            vmem((2, NX, 2, 2, ROWS, S), F32),
-            vmem((2, S, 1280), BF16),
-            vmem((2, S, 1280), BF16),
+            vmem((NX, 2, 2, ROWS, S), F32),
+            vmem((S, 1280), BF16),
+            vmem((S, 1280), BF16),
             dma((NX,)),
             *[dma(shape) for shape in pairs for _ in range(2)],
         ],

time: 145 us -> 140 us (0.966)
  Pallas kernels: 140 us -> 136 us
    pallas_call x1, Pallas kernels: 140 us -> 136 us  [on_device(): pl.pallas_call(kernel, out_shape=(jax.ShapeDtypeStruct((NSUP, ROWS, S), F...]
where the time goes in v3:
time: 140 us
  Pallas kernels  136 us (97%)
  local copies, waits for them, and re-layouts  3.26 us (2%)
    pallas_call x1, Pallas kernels, on_device(): pl.pallas_call(kernel, out_shape=(jax.ShapeDtypeStruct((NSUP, ROWS, S), F...  136 us
    unnamed x2, local copies, waits for them, and re-layouts  3.26 us

profile of v3, /device:TPU:32, one launch (start us, length us, event | category | flops | bytes accessed | tf_op | source)
XLA Modules:
  0.0 140.2 jit_solution(7009364004834636014)
XLA Ops:
  0.6 136.3 %selected_inversion.1 = (f32[3,80,512]{2,1,0:T(8,128)}, f32[3,32,32]{2,1,0:T(8,128)}) custom-call(s32[3,10]{1,0:T(4,128)} %anc.1, f32[1280,1280]{1,0:T(8,128)} %a_hbm.1, f32[3,80,512]{2,1,0:T(8,128)} %panels.1, f32[3,32,32]{2,1,0:T(8,128)} %dinv.1), custom_call_target="tpu_custom_call" | custom-call | tf_op jit(solution)/shard_map/selected_inversion/pallas_call | solution.py:458
  136.9 1.8 %copy.8 = f32[3,80,512]{2,1,0:T(8,128)} copy(f32[3,80,512]{2,1,0:T(8,128)} %get-tuple-element.4) | data formatting | bytes 983040
  138.8 1.4 %copy.9 = f32[3,32,32]{2,1,0:T(8,128)} copy(f32[3,32,32]{2,1,0:T(8,128)} %get-tuple-element.5) | data formatting | bytes 24576

commit v4 on v3

--- a/solution.py
+++ b/solution.py
@@ -15,7 +15,7 @@
 HALF = 256
 UNITS = 2 * NSUP
 PIECE = S // 16
-CROSS = 32
+CROSS = 48
 PROW = ("y_hi", "z")
 PCOL = ("x", "y_lo", "core")
 
@@ -89,7 +89,7 @@
         side = yh if q == 0 else 1 - yh
         low, high = (0, ROWS) if q == 0 else (CROSS, ROWS)
         if t == 3:
-            middle = (low + high) // 2
+            middle = CROSS if q == 0 else CROSS + 8
             low, high = (low, middle) if d == 0 else (middle, high)
         origin = origin_of(d, t + 1 if back else t)
         block = gath.at[u, side * NZ + origin, pl.ds(low, high - low)]
@@ -131,7 +131,7 @@
             across(u, k, True).wait_recv()
 
     first_own(0)
-    for u in range(UNITS):
+    for u in range(3):
         ycopy(u, own).start()
     first_own(1)
     first_other(0)
@@ -311,6 +311,10 @@
         @at(k + 1 < UNITS)
         def _():
             first_own(k + 1)
+
+        @at(k + 2 < UNITS)
+        def _():
+            ycopy(k + 2, own).start()
 
         @at(alive(k - 5))
         def _():

time: 140 us -> 134 us (0.957)
  Pallas kernels: 136 us -> 130 us
    pallas_call x1, Pallas kernels: 136 us -> 130 us  [on_device(): pl.pallas_call(kernel, out_shape=(jax.ShapeDtypeStruct((NSUP, ROWS, S), F...]
where the time goes in v4:
time: 134 us
  Pallas kernels  130 us (97%)
  local copies, waits for them, and re-layouts  3.26 us (2%)
    pallas_call x1, Pallas kernels, on_device(): pl.pallas_call(kernel, out_shape=(jax.ShapeDtypeStruct((NSUP, ROWS, S), F...  130 us
    unnamed x2, local copies, waits for them, and re-layouts  3.26 us

profile of v4, /device:TPU:32, one launch (start us, length us, event | category | flops | bytes accessed | tf_op | source)
XLA Modules:
  0.0 133.9 jit_solution(13349368898086916177)
XLA Ops:
  0.6 130.0 %selected_inversion.1 = (f32[3,80,512]{2,1,0:T(8,128)}, f32[3,32,32]{2,1,0:T(8,128)}) custom-call(s32[3,10]{1,0:T(4,128)} %anc.1, f32[1280,1280]{1,0:T(8,128)} %a_hbm.1, f32[3,80,512]{2,1,0:T(8,128)} %panels.1, f32[3,32,32]{2,1,0:T(8,128)} %dinv.1), custom_call_target="tpu_custom_call" | custom-call | tf_op jit(solution)/shard_map/selected_inversion/pallas_call | solution.py:462
  130.6 1.8 %copy.8 = f32[3,80,512]{2,1,0:T(8,128)} copy(f32[3,80,512]{2,1,0:T(8,128)} %get-tuple-element.4) | data formatting | bytes 983040
  132.5 1.4 %copy.9 = f32[3,32,32]{2,1,0:T(8,128)} copy(f32[3,32,32]{2,1,0:T(8,128)} %get-tuple-element.5) | data formatting | bytes 24576
